TPU v7x, 32 devices: a whole 2x2x4 slice. The times are simulated.
32 devices in a mesh: rad: 8 (over y, x, core), azi: 4 (over z).
Axes of the slice: x: 2, y: 2, z: 4, core: 2. Of those that a mesh axis runs over, the one named last changes fastest.
Arguments:
- positions: float32 [3, 524288], P(None, ('rad', 'azi')), may hold values from 0 to 1
- velocities: float32 [3, 524288], P(None, ('rad', 'azi')), may hold values from -3 to 3
- masses: float32 [524288], P(('rad', 'azi')), may hold values from 0.5 to 2
- neighbours: int32 [4096, 4], P(('rad', 'azi')), may hold values from 0 to 143, as said below
- shear_offsets: int32 [2, 8], replicated, may hold values from 0 to 3
- destinations: int32 [4096], P(('rad', 'azi')), may hold values from 0 to 3, as said below
- deposit_cells: int32 [2, 524288], P(None, ('rad', 'azi')), may hold values from 0 to 4095
- old_potential: float32 [512, 256], P('rad', 'azi'), may hold values from -6 to 6
Outputs:
- migrated: float32 [7, 524288], P(None, ('rad', 'azi'))
- potential: float32 [512, 256], P('rad', 'azi')
Inputs may be any that keep to these rules, and one draw needn't show every extreme that they name: `neighbours`: entries index a device's table of 128 own tiles and 16 ghost tiles; the first entry of each tile's list is the tile itself, and each ghost tile is listed by some tile of every device. `destinations`: one device sends at most 32 tiles to any one azimuthal strip and a device receives at most 128 tiles; in every radial strip one azimuthal strip receives exactly 32 tiles from each device of that radial strip.
All inputs are finite; a program needn't handle non-finite values.
Results may differ from a plain program's by a relative error of at most 0.0003.
Values sent between devices are 32-bit elements; how exact they have to be, the bound alone decides.
A program may use at most 64 MiB of HBM per device.

v0:
```python
import math

import jax
import jax.numpy as jnp
from jax import lax
from jax.sharding import PartitionSpec as P

EDGE = 4
STEPS = 2


TIME_STEP = 0.1
ORBIT_FREQ = 0.3
CONTACT_STIFF = 0.15
INV_WIDTH = 4.0
GRAV_SCALE = 0.01


def shifted(value, axis, steps):
    count = lax.axis_size(axis)
    pairs = [(source, (source + steps) % count) for source in range(count)]
    return lax.ppermute(value, axis, pairs)


def padded_2(cells, sides, width):
    for axis, dim in sides:
        count = lax.axis_size(axis)
        head = lax.slice_in_dim(cells, 0, width, axis=dim)
        tail = lax.slice_in_dim(cells, cells.shape[dim] - width, cells.shape[dim], axis=dim)
        cells = jnp.concatenate(
            [
                lax.ppermute(tail, axis, [(i, (i + 1) % count) for i in range(count)]),
                cells,
                lax.ppermute(head, axis, [((i + 1) % count, i) for i in range(count)]),
            ],
            axis=dim,
        )
    return cells


def contact_forces(own_tiles, table_all, neighbour_rows):
    groups = own_tiles.shape[1] // 4
    own_groups = jnp.transpose(own_tiles.reshape(4, groups, 4, -1), (1, 0, 2, 3))
    row_groups = neighbour_rows.reshape(groups, 4, -1)

    def one_group(group_args):
        own_part, row_part = group_args
        others = jnp.take(table_all, row_part, axis=1)
        offsets = own_part[:3, :, None, :, None] - others[:3, :, :, None, :]
        distance = jnp.sum(offsets * offsets, axis=0)
        weights = others[3][:, :, None, :] * jnp.exp(-INV_WIDTH * distance)
        return CONTACT_STIFF * jnp.sum(offsets * weights[None], axis=(2, 4))

    result = lax.map(one_group, (own_groups, row_groups))
    return jnp.transpose(result, (1, 0, 2, 3)).reshape(3, own_tiles.shape[1], -1)


def phase_table(rows, cols, length):
    row_ids = jnp.arange(rows, dtype=jnp.int32)
    col_ids = jnp.arange(cols, dtype=jnp.int32)
    phases = row_ids[:, None] * col_ids[None, :] % length
    angles = phases.astype(jnp.float32) * (2.0 * jnp.pi / length)
    return (jnp.cos(angles), jnp.sin(angles))


def dft_tables(length):
    first = 1
    for factor in range(1, math.isqrt(length) + 1):
        if length % factor == 0:
            first = factor
    second = length // first
    return (
        first,
        second,
        phase_table(first, first, first),
        phase_table(second, second, second),
        phase_table(second, first, length),
    )


def complex_product(real_part, imag_part, table, sign):
    cosine, sine_table = table
    both = jnp.stack([real_part, imag_part])
    with_cos = jnp.dot(both, cosine, precision=lax.Precision.HIGHEST)
    with_sin = jnp.dot(both, sine_table, precision=lax.Precision.HIGHEST)
    return (with_cos[0] - sign * with_sin[1], with_cos[1] + sign * with_sin[0])


def transform(pencil, tables, inverse):
    first, second, table_first, table_second, twiddle = tables
    length = first * second
    sign = 1.0 if inverse else -1.0
    rows = pencil.shape[1]
    real_part = jnp.swapaxes(pencil[0].reshape(rows, first, second), 1, 2)
    imag_part = jnp.swapaxes(pencil[1].reshape(rows, first, second), 1, 2)
    real_part, imag_part = complex_product(real_part, imag_part, table_first, sign)
    twist_cos, twist_sin = twiddle
    twist_sin = sign * twist_sin
    real_part, imag_part = (
        real_part * twist_cos - imag_part * twist_sin,
        imag_part * twist_cos + real_part * twist_sin,
    )
    real_part = jnp.swapaxes(real_part, 1, 2)
    imag_part = jnp.swapaxes(imag_part, 1, 2)
    real_part, imag_part = complex_product(real_part, imag_part, table_second, sign)
    real_part = jnp.swapaxes(real_part, 1, 2).reshape(rows, length)
    imag_part = jnp.swapaxes(imag_part, 1, 2).reshape(rows, length)
    if inverse:
        return jnp.stack([real_part / length, imag_part / length])
    return jnp.stack([real_part, imag_part])


def green_values(wave_x, wave_y, size_x, size_y):
    eigen_x = 4.0 * jnp.sin(jnp.pi * wave_x.astype(jnp.float32) / size_x) ** 2
    eigen_y = 4.0 * jnp.sin(jnp.pi * wave_y.astype(jnp.float32) / size_y) ** 2
    lam_grid = eigen_x[:, None] + eigen_y[None, :]
    at_zero = (wave_x[:, None] == 0) & (wave_y[None, :] == 0)
    return jnp.where(at_zero, 0.0, -GRAV_SCALE / jnp.where(at_zero, 1.0, lam_grid))


def along_radial(blocks, tables, inverse):
    turned = jnp.swapaxes(blocks, 1, 2)
    pencil = lax.all_to_all(turned, "rad", split_axis=1, concat_axis=2, tiled=True)
    pencil = transform(pencil, tables, inverse)
    turned = lax.all_to_all(pencil, "rad", split_axis=2, concat_axis=1, tiled=True)
    return jnp.swapaxes(turned, 1, 2)


def solve_potential(density, tables_x, tables_y, rad_place, azi_place, rad_count, azi_count):
    grid_x, grid_y = density.shape
    size_x = grid_x * rad_count
    size_y = grid_y * azi_count
    blocks = jnp.stack([density, jnp.zeros_like(density)])
    blocks = along_radial(blocks, tables_x, False)
    pencil = lax.all_to_all(blocks, "azi", split_axis=1, concat_axis=2, tiled=True)
    pencil = transform(pencil, tables_y, False)
    rows_each = grid_x // azi_count
    wave_x = rad_place * grid_x + azi_place * rows_each + jnp.arange(rows_each, dtype=jnp.int32)
    wave_y = jnp.arange(size_y, dtype=jnp.int32)
    pencil = pencil * green_values(wave_x, wave_y, size_x, size_y)[None]
    pencil = transform(pencil, tables_y, True)
    blocks = lax.all_to_all(pencil, "azi", split_axis=2, concat_axis=1, tiled=True)
    blocks = along_radial(blocks, tables_x, True)
    return blocks[0]


def ghost_table(carried, offsets_now, rad_place, azi_place, rad_count, azi_count):
    from_below = shifted(carried[:, EDGE : 2 * EDGE], "rad", 1)
    from_above = shifted(carried[:, :EDGE], "rad", -1)
    amount_below = offsets_now[rad_place]
    amount_above = (azi_count - offsets_now[(rad_place + 1) % rad_count]) % azi_count
    stacked = jnp.stack([from_below, from_above])
    all_rows = lax.all_gather(stacked[None], "azi", axis=0, tiled=True)
    source_below = (azi_place - amount_below) % azi_count
    source_above = (azi_place - amount_above) % azi_count
    sheared_below = lax.dynamic_index_in_dim(all_rows, source_below, 0, keepdims=False)[0]
    sheared_above = lax.dynamic_index_in_dim(all_rows, source_above, 0, keepdims=False)[1]
    from_left = shifted(carried[:, 3 * EDGE : 4 * EDGE], "azi", 1)
    from_right = shifted(carried[:, 2 * EDGE : 3 * EDGE], "azi", -1)
    sheared_below = sheared_below.at[0].add(-1.0)
    sheared_above = sheared_above.at[0].add(1.0)
    from_left = from_left.at[1].add(-1.0)
    from_right = from_right.at[1].add(1.0)
    return jnp.concatenate([carried, sheared_below, sheared_above, from_left, from_right], axis=1)


def local(
    positions,
    velocities,
    masses,
    neighbours,
    shear_offsets,
    destinations,
    deposit_cells,
    old_potential,
):
    rad_count = lax.axis_size("rad")
    azi_count = lax.axis_size("azi")
    rad_place = lax.axis_index("rad")
    azi_place = lax.axis_index("azi")
    tile_count = neighbours.shape[0]
    tile_size = positions.shape[1] // tile_count
    grid_x, grid_y = old_potential.shape
    tables_x = dft_tables(grid_x * rad_count)
    tables_y = dft_tables(grid_y * azi_count)
    place = positions
    speed = velocities
    potential_now = old_potential
    strip_x = (rad_place - rad_count // 2).astype(jnp.float32)
    for step_index in range(STEPS):
        cells_now = deposit_cells[step_index]
        padded = padded_2(potential_now, (("rad", 0), ("azi", 1)), 1)
        grad_x = -(padded[2:, 1:-1] - padded[:-2, 1:-1]) * 0.5
        grad_y = -(padded[1:-1, 2:] - padded[1:-1, :-2]) * 0.5
        grad_field = jnp.stack([grad_x, grad_y]).reshape(2, -1)
        gravity = jnp.take(grad_field, cells_now, axis=1)
        density = jax.ops.segment_sum(masses, cells_now, num_segments=grid_x * grid_y).reshape(
            grid_x, grid_y
        )
        next_potential = solve_potential(
            density, tables_x, tables_y, rad_place, azi_place, rad_count, azi_count
        )
        carried = jnp.concatenate([place, masses[None]], axis=0).reshape(4, tile_count, tile_size)
        table_all = ghost_table(
            carried, shear_offsets[step_index], rad_place, azi_place, rad_count, azi_count
        )
        forces = contact_forces(carried, table_all, neighbours).reshape(3, -1)
        tidal_x = place[0] + strip_x
        accel = jnp.stack(
            [
                forces[0]
                + gravity[0]
                + 2.0 * ORBIT_FREQ * speed[1]
                + 3.0 * ORBIT_FREQ**2 * tidal_x,
                forces[1] + gravity[1] - 2.0 * ORBIT_FREQ * speed[0],
                forces[2] - ORBIT_FREQ**2 * (place[2] - 0.5),
            ]
        )
        speed = speed + TIME_STEP * accel
        place = place + TIME_STEP * speed
        potential_now = next_potential
    final_state = jnp.concatenate([place, speed, masses[None]], axis=0).reshape(
        7, tile_count, tile_size
    )
    slot_cap = tile_count // 4
    capacity = slot_cap * azi_count
    strip_ids = jnp.arange(azi_count, dtype=jnp.int32)
    signed = (azi_place - destinations + azi_count // 2) % azi_count - azi_count // 2
    final_state = final_state.at[1].add(signed.astype(jnp.float32)[:, None])
    hit_table = (destinations[:, None] == strip_ids[None, :]).astype(jnp.int32)
    earlier = jnp.cumsum(hit_table, axis=0) - hit_table
    rank_slot = jnp.sum(earlier * hit_table, axis=1)
    target = destinations * slot_cap + rank_slot
    select = (jnp.arange(capacity, dtype=jnp.int32)[:, None] == target[None, :]).astype(jnp.float32)
    packed = jnp.einsum("st,ctp->csp", select, final_state, precision=lax.Precision.HIGHEST)
    packed = packed.reshape(7, azi_count, slot_cap * tile_size)
    arrived = lax.all_to_all(packed, "azi", split_axis=1, concat_axis=1, tiled=True)
    return (arrived.reshape(7, -1), potential_now)


def solution(mesh):
    placed = (
        P(None, ("rad", "azi")),
        P(None, ("rad", "azi")),
        P(("rad", "azi")),
        P(("rad", "azi"), None),
        P(),
        P(("rad", "azi")),
        P(None, ("rad", "azi")),
        P("rad", "azi"),
    )
    return jax.shard_map(
        local,
        mesh=mesh,
        in_specs=placed,
        out_specs=(P(None, ("rad", "azi")), P("rad", "azi")),
        check_vma=False,
    )
```

profile of v0, /device:TPU:0, one launch (start us, length us, event | category | flops | bytes accessed | tf_op | source)
XLA Modules:
  0.0 645.0 jit_solution(10775512302935554638)
XLA Ops:
  1.8 86.1 %scatter_custom_fusion.1 = f32[4096]{0:T(1024)S(1)} fusion(s32[16384]{0:T(1024)S(1)} %bitcast.670, f32[16384]{0:T(1024)} %param.36, f32[]{:T(128)} %constant.431.clone.1), kind=kCustom, calls=%fused_computation.373 | custom fusion | flops 16384 | bytes 16896 | tf_op jit(solution)/shard_map/scatter-add | solution.py:197
  88.8 5.2 all-to-all-start.7
  98.4 3.6 collective-permute-start.3
  111.0 85.8 %scatter_custom_fusion = f32[4096]{0:T(1024)S(1)} fusion(s32[16384]{0:T(1024)S(1)} %bitcast.669, f32[16384]{0:T(1024)S(1)} %copy-done.1, f32[]{:T(128)} %constant.431.clone.1), kind=kCustom, calls=%fused_computation.375 | custom fusion | flops 16384 | bytes 16388 | tf_op jit(solution)/shard_map/scatter-add | solution.py:197
  205.8 54.8 %gather_fusion.2 = f32[16384,2]{1,0:T(8,128)} fusion(f32[2,4096]{0,1:T(8,128)S(1)} %copy.803, s32[16384]{0:T(1024)S(1)} %fusion.106), kind=kCustom, calls=%fused_computation.1.clone | custom fusion | bytes 327680 | tf_op jit(solution)/shard_map/jit(_take)/gather | solution.py:196
  260.6 5.3 copy.804
  266.1 13.1 %all-gather = f32[8,4,4,128]{3,2,1,0:T(4,128)S(1)} all-gather(f32[2,4,4,128]{3,2,1,0:T(4,128)S(1)} %pad_maximum_fusion.75), channel_id=2, replica_groups=mesh['rad'=8,'azi'=4] {'azi'}, dimensions={0}, use_global_device_ids=true | all-gather | bytes 81920 | tf_op jit(solution)/shard_map/all_gather | solution.py:153
  279.5 68.4 %while.29 = (s32[]{:T(128)}, f32[32,3,4,128]{3,2,1,0:T(4,128)S(1)}, f32[32,4,4,128]{3,2,0,1:T(4,128)S(1)}, s32[32,4,4]{2,1,0:T(4,128)S(1)}, f32[4,144,128]{2,0,1:T(4,128)S(1)}, /*index=5*/s32[]{:T(128)}) while((s32[]{:T(128)}, f32[32,3,4,128]{3,2,1,0:T(4,128)S(1)}, f32[32,4,4,128]{3,2,0,1:T(4,128)S(1)}, s32[32,4,4]{2,1,0:T(4,128)S(1)}, ...), condition=%wide.region_3.5_spmd, body=%wide.region_0.4_spmd.sunk | while | flops 4990050 | bytes 4512241 | solution.py:54
  353.8 5.0 collective-permute-done.10
  358.8 13.1 %all-gather.1 = f32[8,4,4,128]{3,2,1,0:T(4,128)S(1)} all-gather(f32[2,4,4,128]{3,2,1,0:T(4,128)S(1)} %pad_maximum_fusion.76), channel_id=3, replica_groups=mesh['rad'=8,'azi'=4] {'azi'}, dimensions={0}, use_global_device_ids=true | all-gather | bytes 81920 | tf_op jit(solution)/shard_map/all_gather | solution.py:153
  372.0 3.5 all-to-all-start
  393.5 3.3 all-to-all-start.8
  410.5 3.5 all-to-all-start.9
  416.0 3.5 all-to-all-done.9
  436.5 4.0 all-to-all-done.3
  440.5 3.5 all-to-all-start.10
  444.1 68.0 %while.30 = (s32[]{:T(128)}, f32[32,3,4,128]{3,2,1,0:T(4,128)S(1)}, f32[32,4,4,128]{3,2,1,0:T(4,128)S(1)}, s32[32,4,4]{2,1,0:T(4,128)S(1)}, f32[4,144,128]{2,0,1:T(4,128)S(1)}, /*index=5*/s32[]{:T(128)}) while((s32[]{:T(128)}, f32[32,3,4,128]{3,2,1,0:T(4,128)S(1)}, f32[32,4,4,128]{3,2,1,0:T(4,128)S(1)}, s32[32,4,4]{2,1,0:T(4,128)S(1)}, ...), condition=%wide.region_7.10_spmd, body=%wide.region_4.9_spmd.sunk | while | flops 4990050 | bytes 4495857 | solution.py:54
  514.1 3.3 all-to-all-start.4
  539.3 4.8 all-to-all-done.5
  550.2 3.8 collective-permute-start.14
  560.6 54.8 %gather_fusion.3 = f32[16384,2]{1,0:T(8,128)} fusion(f32[2,4096]{0,1:T(8,128)S(1)} %copy.860, s32[16384]{0:T(1024)S(1)} %fusion.107), kind=kCustom, calls=%fused_computation.3.clone | custom fusion | bytes 327680 | tf_op jit(solution)/shard_map/jit(_take)/gather | solution.py:196
  615.4 5.3 copy.861
  623.9 4.7 all-to-all-start.6
  631.0 12.7 %all-to-all-done.6 = f32[7,4,4096]{2,0,1:T(8,128)S(1)} async-done(((f32[7,4,4096]{2,0,1:T(8,128)}), f32[7,4,4096]{2,0,1:T(8,128)S(1)}, u32[]{:S(2)}, u32[]{:S(2)}) %all-to-all-start.6) | async-done | bytes 458784 | tf_op jit(solution)/shard_map/all_to_all | solution.py:237
  (1145 shorter events, 251.4 us)
Async XLA Ops:
  88.8 283.2 %all-to-all-start.7 = ((f32[8,1,1024]{2,1,0:T(1,128)}), f32[8,1,1024]{2,1,0:T(1,128)S(1)}, u32[]{:S(2)}, u32[]{:S(2)}) async-start(f32[8,1,1024]{2,1,0:T(1,128)} %reshape.913), calls=%async_computation.7 | async-start | bytes 65536 | tf_op jit(solution)/shard_map/all_to_all | solution.py:123
  95.7 170.3 %collective-permute-start = (f32[4,4,128]{2,1,0:T(4,128)S(1)}, f32[4,4,128]{2,1,0:T(4,128)S(1)}, u32[]{:S(2)}, u32[]{:S(2)}) collective-permute-start(f32[4,4,128]{2,1,0:T(4,128)S(1)} %get-tuple-element.301), channel_id=1, source_target_pairs={{0,4},{4,8},{8,12},{12,16},{16,20},{20,24},{24,28},{28,0},{1,5},{5... | collective-permute-start | bytes 24584 | tf_op jit(solution)/shard_map/ppermute | solution.py:22
  96.2 169.8 %collective-permute-start.1 = (f32[4,4,128]{2,1,0:T(4,128)S(1)}, f32[4,4,128]{2,1,0:T(4,128)S(1)}, u32[]{:S(2)}, u32[]{:S(2)}) collective-permute-start(f32[4,4,128]{2,1,0:T(4,128)S(1)} %get-tuple-element.302), channel_id=1, source_target_pairs={{0,28},{4,0},{8,4},{12,8},{16,12},{20,16},{24,20},{28,24},{1,29},{... | collective-permute-start | bytes 24584 | tf_op jit(solution)/shard_map/ppermute | solution.py:22
  98.4 180.7 %collective-permute-start.3 = (f32[4,4,128]{2,1,0:T(4,128)S(1)}, f32[4,4,128]{2,1,0:T(4,128)S(1)}, u32[]{:S(2)}, u32[]{:S(2)}) collective-permute-start(f32[4,4,128]{2,1,0:T(4,128)S(1)} %get-tuple-element.300), channel_id=1, source_target_pairs={{0,3},{1,0},{2,1},{3,2},{4,7},{5,4},{6,5},{7,6},{8,11},{9,8},{10,9... | collective-permute-start | bytes 24584 | tf_op jit(solution)/shard_map/ppermute | solution.py:22
  102.8 95.9 %collective-permute-start.4 = (f32[1,64]{0,1:T(8,128)S(1)}, f32[1,64]{0,1:T(8,128)S(1)}, u32[]{:S(2)}, u32[]{:S(2)}) collective-permute-start(f32[1,64]{0,1:T(8,128)S(1)} %copy.796), channel_id=1, source_target_pairs={{4,0},{8,4},{12,8},{16,12},{20,16},{24,20},{28,24},{0,28},{5,1},{9... | collective-permute-start | bytes 776 | tf_op jit(solution)/shard_map/ppermute | solution.py:34
  103.1 95.6 %collective-permute-start.5 = (f32[1,64]{0,1:T(8,128)S(1)}, f32[1,64]{0,1:T(8,128)S(1)}, u32[]{:S(2)}, u32[]{:S(2)}) collective-permute-start(f32[1,64]{0,1:T(8,128)S(1)} %copy.798), channel_id=1, source_target_pairs={{0,4},{4,8},{8,12},{12,16},{16,20},{20,24},{24,28},{28,0},{1,5},{5... | collective-permute-start | bytes 776 | tf_op jit(solution)/shard_map/ppermute | solution.py:32
  199.3 5.4 collective-permute-start.7
  202.4 76.8 %collective-permute-start.2 = (f32[4,4,128]{2,1,0:T(4,128)S(1)}, f32[4,4,128]{2,1,0:T(4,128)S(1)}, u32[]{:S(2)}, u32[]{:S(2)}) collective-permute-start(f32[4,4,128]{2,1,0:T(4,128)S(1)} %get-tuple-element.303), channel_id=1, source_target_pairs={{0,1},{1,2},{2,3},{3,0},{4,5},{5,6},{6,7},{7,4},{8,9},{9,10},{10,1... | collective-permute-start | bytes 24584 | tf_op jit(solution)/shard_map/ppermute | solution.py:22
  350.7 8.2 %collective-permute-start.8 = (f32[4,4,128]{2,1,0:T(4,128)S(1)}, f32[4,4,128]{2,1,0:T(4,128)S(1)}, u32[]{:S(2)}, u32[]{:S(2)}) collective-permute-start(f32[4,4,128]{2,1,0:T(4,128)S(1)} %get-tuple-element.296), channel_id=1, source_target_pairs={{0,4},{4,8},{8,12},{12,16},{16,20},{20,24},{24,28},{28,0},{1,5},{5... | collective-permute-start | bytes 24584 | tf_op jit(solution)/shard_map/ppermute | solution.py:22
  350.7 8.1 %collective-permute-start.9 = (f32[4,4,128]{2,1,0:T(4,128)S(1)}, f32[4,4,128]{2,1,0:T(4,128)S(1)}, u32[]{:S(2)}, u32[]{:S(2)}) collective-permute-start(f32[4,4,128]{2,1,0:T(4,128)S(1)} %get-tuple-element.297), channel_id=1, source_target_pairs={{0,28},{4,0},{8,4},{12,8},{16,12},{20,16},{24,20},{28,24},{1,29},{... | collective-permute-start | bytes 24584 | tf_op jit(solution)/shard_map/ppermute | solution.py:22
  353.4 5.4 collective-permute-start.10
  372.0 8.3 %all-to-all-start = ((f32[8,1,1024]{2,1,0:T(1,128)}), f32[8,1,1024]{2,1,0:T(1,128)S(1)}, u32[]{:S(2)}, u32[]{:S(2)}) async-start(f32[8,1,1024]{2,1,0:T(1,128)} %reshape.901), calls=%async_computation | async-start | bytes 65536 | tf_op jit(solution)/shard_map/all_to_all | solution.py:123
  385.4 8.1 %all-to-all-start.1 = ((f32[8,1,1024]{2,1,0:T(1,128)}), f32[8,1,1024]{2,1,0:T(1,128)S(1)}, u32[]{:S(2)}, u32[]{:S(2)}) async-start(f32[8,1,1024]{2,1,0:T(1,128)} %reshape.903), calls=%async_computation.1 | async-start | bytes 65536 | tf_op jit(solution)/shard_map/all_to_all | solution.py:125
  393.5 8.1 %all-to-all-start.8 = ((f32[8,1,1024]{2,1,0:T(1,128)}), f32[8,1,1024]{2,1,0:T(1,128)S(1)}, u32[]{:S(2)}, u32[]{:S(2)}) async-start(f32[8,1,1024]{2,1,0:T(1,128)} %reshape.915), calls=%async_computation.8 | async-start | bytes 65536 | tf_op jit(solution)/shard_map/all_to_all | solution.py:125
  401.6 8.9 %all-to-all-start.2 = ((f32[4,1,2048]{2,1,0:T(1,128)}), f32[4,1,2048]{2,1,0:T(1,128)S(1)}, u32[]{:S(2)}, u32[]{:S(2)}) async-start(f32[4,1,2048]{2,1,0:T(1,128)} %reshape.905), calls=%async_computation.2 | async-start | bytes 65536 | tf_op jit(solution)/shard_map/all_to_all | solution.py:135
  410.5 9.1 %all-to-all-start.9 = ((f32[4,1,2048]{2,1,0:T(1,128)}), f32[4,1,2048]{2,1,0:T(1,128)S(1)}, u32[]{:S(2)}, u32[]{:S(2)}) async-start(f32[4,1,2048]{2,1,0:T(1,128)} %reshape.917), calls=%async_computation.9 | async-start | bytes 65536 | tf_op jit(solution)/shard_map/all_to_all | solution.py:135
  431.6 8.9 %all-to-all-start.3 = ((f32[4,1,2048]{2,1,0:T(1,128)}), f32[4,1,2048]{2,1,0:T(1,128)S(1)}, u32[]{:S(2)}, u32[]{:S(2)}) async-start(f32[4,1,2048]{2,1,0:T(1,128)} %reshape.907), calls=%async_computation.3 | async-start | bytes 65536 | tf_op jit(solution)/shard_map/all_to_all | solution.py:142
  440.5 73.6 %all-to-all-start.10 = ((f32[4,1,2048]{2,1,0:T(1,128)}), f32[4,1,2048]{2,1,0:T(1,128)S(1)}, u32[]{:S(2)}, u32[]{:S(2)}) async-start(f32[4,1,2048]{2,1,0:T(1,128)} %reshape.919), calls=%async_computation.10 | async-start | bytes 65536 | tf_op jit(solution)/shard_map/all_to_all | solution.py:142
  514.1 8.1 %all-to-all-start.4 = ((f32[8,1,1024]{2,1,0:T(1,128)}), f32[8,1,1024]{2,1,0:T(1,128)S(1)}, u32[]{:S(2)}, u32[]{:S(2)}) async-start(f32[8,1,1024]{2,1,0:T(1,128)} %reshape.909), calls=%async_computation.4 | async-start | bytes 65536 | tf_op jit(solution)/shard_map/all_to_all | solution.py:123
  522.3 8.1 %all-to-all-start.11 = ((f32[8,1,1024]{2,1,0:T(1,128)}), f32[8,1,1024]{2,1,0:T(1,128)S(1)}, u32[]{:S(2)}, u32[]{:S(2)}) async-start(f32[8,1,1024]{2,1,0:T(1,128)} %reshape.921), calls=%async_computation.11 | async-start | bytes 65536 | tf_op jit(solution)/shard_map/all_to_all | solution.py:123
  535.9 8.1 %all-to-all-start.5 = ((f32[8,1,1024]{2,1,0:T(1,128)}), f32[8,1,1024]{2,1,0:T(1,128)S(1)}, u32[]{:S(2)}, u32[]{:S(2)}) async-start(f32[8,1,1024]{2,1,0:T(1,128)} %reshape.911), calls=%async_computation.5 | async-start | bytes 65536 | tf_op jit(solution)/shard_map/all_to_all | solution.py:125
  550.2 8.8 %collective-permute-start.14 = (f32[66,1]{0,1:T(1,128)S(1)}, f32[66,1]{0,1:T(1,128)S(1)}, u32[]{:S(2)}, u32[]{:S(2)}) collective-permute-start(f32[66,1]{0,1:T(1,128)S(1)} %get-tuple-element.314), channel_id=1, source_target_pairs={{1,0},{2,1},{3,2},{0,3},{5,4},{6,5},{7,6},{4,7},{9,8},{10,9},{11,1... | collective-permute-start | bytes 800 | tf_op jit(solution)/shard_map/ppermute | solution.py:34
  555.7 68.3 %all-to-all-start.12 = ((f32[8,1,1024]{2,1,0:T(1,128)}), f32[8,1,1024]{2,1,0:T(1,128)S(1)}, u32[]{:S(2)}, u32[]{:S(2)}) async-start(f32[8,1,1024]{2,1,0:T(1,128)} %reshape.923), calls=%async_computation.12 | async-start | bytes 65536 | tf_op jit(solution)/shard_map/all_to_all | solution.py:125
  623.9 19.8 %all-to-all-start.6 = ((f32[7,4,4096]{2,0,1:T(8,128)}), f32[7,4,4096]{2,0,1:T(8,128)S(1)}, u32[]{:S(2)}, u32[]{:S(2)}) async-start(f32[7,4,4096]{2,0,1:T(8,128)} %copy.867), calls=%async_computation.6 | async-start | bytes 1048576 | tf_op jit(solution)/shard_map/all_to_all | solution.py:237
  (10 other events, 662.4 us)
where the time goes:
time: 654 us; the launch traced here: 645 us
  other arithmetic  272 us (42%)
  local copies, waits for them, and re-layouts  203 us (31%)
  starting transfers between devices  65 us (10%)
  waiting for transfers between devices  54.6 us (8%)
  blocking collectives  26.3 us (4%)
  matrix products  13.4 us (2%)
    scatter-add x2, other arithmetic, local(): jax.ops.segment_sum(masses, cells_now, num_segments=grid_x * grid_y)  172 us
    gather x4, local copies, waits for them, and re-layouts, local(): gravity = jnp.take(grad_field, cells_now, axis=1)  120 us
    reduce_sum x64, other arithmetic, one_group(): return CONTACT_STIFF * jnp.sum(offsets * weights[None], axis=(2, 4))  44.9 us
    gather x64, local copies, waits for them, and re-layouts, one_group(): others = jnp.take(table_all, row_part, axis=1)  37.6 us
    all_gather x2, blocking collectives, ghost_table(): all_rows = lax.all_gather(stacked[None], 'azi', axis=0, tiled=True)  26.3 us
    reduce_sum x64, other arithmetic, one_group(): distance = jnp.sum(offsets * offsets, axis=0)  24.5 us
    unnamed x42, local copies, waits for them, and re-layouts  19.9 us
    all_to_all x4, starting transfers between devices, along_radial(): lax.all_to_all(turned, 'rad', split_axis=1, concat_axis=2, tiled=True)  15.4 us
  transfers between devices with their start and end apart: 29, of which 16 were waited for; matrix products, arithmetic and copies ran while one was open for 58% of the time, Pallas kernels for 0%

commit v1 on v0

v1 whole, which is shorter than its diff:
```python
import functools
import math

import jax
import jax.numpy as jnp
import numpy as np
from jax import lax
from jax.experimental import pallas as pl
from jax.experimental.pallas import tpu as pltpu
from jax.sharding import PartitionSpec as P

EDGE = 4
LINKS = 4
STEPS = 2
TIME_STEP = 0.1
ORBIT_FREQ = 0.3
CONTACT_STIFF = 0.15
INV_WIDTH = 4.0
GRAV_SCALE = 0.01
SCALE = math.sqrt(INV_WIDTH * math.log2(math.e))
MESH = pl.DeviceIdType.MESH
VMEM = pl.BlockSpec(memory_space=pltpu.VMEM)
SMEM = pl.BlockSpec(memory_space=pltpu.SMEM)


def real_basis(length):
    half = length // 2
    waves = np.concatenate([np.arange(half + 1), np.arange(1, half)])
    phase = (waves[:, None] * np.arange(length)[None, :]) % length
    angle = phase * (2.0 * np.pi / length)
    rows = np.where(np.arange(length)[:, None] <= half, np.cos(angle), np.sin(angle))
    norm = np.where((waves == 0) | (waves == half), 1.0, 2.0)
    return rows * np.sqrt(norm / length)[:, None], waves


def split_two(value):
    high = value.astype(jnp.bfloat16).astype(jnp.float32)
    return high, value - high


def cell_parts(cells, grid_y):
    if grid_y & (grid_y - 1) == 0:
        bits = grid_y.bit_length() - 1
        return lax.shift_right_logical(cells, bits), cells & (grid_y - 1)
    return cells // grid_y, cells % grid_y


def one_hot(ids, rows):
    return lax.broadcasted_iota(jnp.int32, (rows, ids.shape[1]), 0) == ids


def last_dims(left, right):
    return lax.dot_general(
        left, right, (((1,), (1,)), ((), ())), preferred_element_type=jnp.float32
    )


def density_kernel(grid_x, grid_y, chunk, cells_ref, mass_ref, out_ref):
    count = mass_ref.shape[1] // chunk

    def body(index, sums):
        at = pl.ds(pl.multiple_of(index * chunk, chunk), chunk)
        high, low = split_two(mass_ref[:, at])
        new = []
        for step in range(STEPS):
            cell_x, cell_y = cell_parts(cells_ref[step : step + 1, at], grid_y)
            hit = one_hot(cell_x, grid_x)
            left = jnp.concatenate(
                [jnp.where(hit, high, 0.0), jnp.where(hit, low, 0.0)], axis=0
            ).astype(jnp.bfloat16)
            right = jnp.where(one_hot(cell_y, grid_y), 1.0, 0.0).astype(jnp.bfloat16)
            new.append(sums[step] + last_dims(left, right))
        return tuple(new)

    zero = jnp.zeros((2 * grid_x, grid_y), jnp.float32)
    sums = lax.fori_loop(0, count, body, (zero,) * STEPS)
    for step in range(STEPS):
        out_ref[step] = sums[step][:grid_x] + sums[step][grid_x:]


def densities(cells, mass_row, grid_x, grid_y):
    return pl.pallas_call(
        functools.partial(density_kernel, grid_x, grid_y, 1024),
        out_shape=jax.ShapeDtypeStruct((STEPS, grid_x, grid_y), jnp.float32),
        in_specs=[VMEM, VMEM],
        out_specs=VMEM,
        name="deposit",
        cost_estimate=pl.CostEstimate(flops=4 * 10**8, bytes_accessed=3 * 10**5, transcendentals=0),
    )(cells, mass_row)


def exchange_kernel(rad_count, azi_count, edges_ref, out_ref, send_sem, recv_sem):
    rad = lax.axis_index("rad")
    azi = lax.axis_index("azi")
    above = lax.rem(rad + 1, rad_count)
    below = lax.rem(rad + rad_count - 1, rad_count)
    right = lax.rem(azi + 1, azi_count)
    left = lax.rem(azi + azi_count - 1, azi_count)
    partners = [(above, other) for other in range(azi_count)]
    partners += [(below, other) for other in range(azi_count)]
    partners += [(rad, right), (rad, left)]
    barrier = pltpu.get_barrier_semaphore()
    for partner in partners:
        pl.semaphore_signal(barrier, inc=1, device_id=partner, device_id_type=MESH)
    pl.semaphore_wait(barrier, len(partners))
    copies = []
    for index, partner in enumerate(partners):
        if index < azi_count:
            source, slot = 0, azi
        elif index < 2 * azi_count:
            source, slot = 1, azi_count + azi
        else:
            source = slot = index - 2 * azi_count
            source, slot = 2 + source, 2 * azi_count + slot
        copy = pltpu.make_async_remote_copy(
            src_ref=edges_ref.at[source],
            dst_ref=out_ref.at[slot],
            send_sem=send_sem.at[index],
            recv_sem=recv_sem.at[slot],
            device_id=partner,
            device_id_type=MESH,
        )
        copy.start()
        copies.append(copy)
    for index, partner in enumerate(partners):
        pltpu.make_async_remote_copy(
            src_ref=edges_ref.at[0],
            dst_ref=out_ref.at[index],
            send_sem=send_sem.at[index],
            recv_sem=recv_sem.at[index],
            device_id=partner,
            device_id_type=MESH,
        ).wait_recv()
    for copy in copies:
        copy.wait_send()


def exchange(edges, rad_count, azi_count, ident):
    slots = 2 * azi_count + 2
    return pl.pallas_call(
        functools.partial(exchange_kernel, rad_count, azi_count),
        out_shape=jax.ShapeDtypeStruct((slots,) + edges.shape[1:], jnp.float32),
        in_specs=[VMEM],
        out_specs=VMEM,
        scratch_shapes=[pltpu.SemaphoreType.DMA((slots,)), pltpu.SemaphoreType.DMA((slots,))],
        compiler_params=pltpu.CompilerParams(collective_id=ident, has_side_effects=True),
        name=f"exchange_{ident}",
        cost_estimate=pl.CostEstimate(flops=0, bytes_accessed=10**7, transcendentals=0),
    )(edges)


def migrate_kernel(azi_count, packed_ref, out_ref, send_sem, recv_sem, local_sem):
    rad = lax.axis_index("rad")
    azi = lax.axis_index("azi")
    width = packed_ref.shape[1] // azi_count
    others = [lax.rem(azi + hop, azi_count) for hop in range(1, azi_count)]
    barrier = pltpu.get_barrier_semaphore()
    for other in others:
        pl.semaphore_signal(barrier, inc=1, device_id=(rad, other), device_id_type=MESH)
    pl.semaphore_wait(barrier, len(others))
    mine = pl.ds(pl.multiple_of(azi * width, width), width)
    copies = []
    for index, other in enumerate(others):
        theirs = pl.ds(pl.multiple_of(other * width, width), width)
        copy = pltpu.make_async_remote_copy(
            src_ref=packed_ref.at[:, theirs],
            dst_ref=out_ref.at[:, mine],
            send_sem=send_sem.at[index],
            recv_sem=recv_sem.at[index],
            device_id=(rad, other),
            device_id_type=MESH,
        )
        copy.start()
        copies.append(copy)
    own = pltpu.make_async_copy(packed_ref.at[:, mine], out_ref.at[:, mine], local_sem)
    own.start()
    own.wait()
    for copy in copies:
        copy.wait()


def migrate(packed, azi_count, ident):
    return pl.pallas_call(
        functools.partial(migrate_kernel, azi_count),
        out_shape=jax.ShapeDtypeStruct(packed.shape, jnp.float32),
        in_specs=[VMEM],
        out_specs=VMEM,
        scratch_shapes=[
            pltpu.SemaphoreType.DMA((azi_count - 1,)),
            pltpu.SemaphoreType.DMA((azi_count - 1,)),
            pltpu.SemaphoreType.DMA,
        ],
        compiler_params=pltpu.CompilerParams(collective_id=ident, has_side_effects=True),
        name="migrate",
        cost_estimate=pl.CostEstimate(flops=0, bytes_accessed=4 * 10**7, transcendentals=0),
    )(packed)


def step_kernel(
    step, azi_count, rad_count, tile_count, grid_y, last, unroll,
    nbr_ref, slot_ref, target_ref, pos_ref, vel_ref, mass_ref, recv_ref, cells_ref, field_ref,
    *rest,
):
    if last:
        out_ref, table_ref, terms_ref, field_two_ref = rest
    else:
        pos_out, vel_out, table_ref, terms_ref, field_two_ref = rest
    tile = pos_ref.shape[1] // tile_count
    strip_x = (lax.axis_index("rad") - rad_count // 2).astype(jnp.float32)
    grid_x = field_ref.shape[1]
    high, low = split_two(field_ref[...])
    field_two_ref[...] = jnp.concatenate([high, low], axis=1).astype(jnp.bfloat16)
    if last:
        out_ref[...] = jnp.zeros_like(out_ref)

    def enter(index, place, mass):
        table_ref[index] = jnp.concatenate(
            [place * SCALE, jnp.zeros((5, tile), jnp.float32)], axis=0
        )
        rows = jnp.concatenate([mass, place * mass], axis=0)
        first = rows.astype(jnp.bfloat16).astype(jnp.float32)
        second = (rows - first).astype(jnp.bfloat16).astype(jnp.float32)
        third = rows - first - second
        terms_ref[index] = jnp.concatenate(
            [first, second, third, jnp.zeros((4, tile), jnp.float32)], axis=0
        ).astype(jnp.bfloat16)

    def own_entry(index, carry):
        at = pl.ds(pl.multiple_of(index * tile, tile), tile)
        enter(index, pos_ref[:, at], mass_ref[:, at])
        return carry

    lax.fori_loop(0, tile_count, own_entry, 0, unroll=4)
    axis_ids = lax.broadcasted_iota(jnp.int32, (3, tile), 0)
    shifts = ((0, -1.0), (0, 1.0), (1, -1.0), (1, 1.0))
    for side, (axis, amount) in enumerate(shifts):
        slot = slot_ref[side]
        for part in range(EDGE):
            block = recv_ref[slot, 0:4, part * tile : (part + 1) * tile]
            shift = jnp.where(axis_ids == axis, amount, 0.0)
            enter(tile_count + side * EDGE + part, block[0:3] + shift, block[3:4])

    def one_tile(index):
        at = pl.ds(pl.multiple_of(index * tile, tile), tile)
        turned = jnp.transpose(table_ref[index])
        own = [jnp.broadcast_to(turned[:, axis : axis + 1], (tile, tile)) for axis in range(3)]
        weights, terms = [], []
        for link in range(LINKS):
            other = nbr_ref[index * LINKS + link]
            rows = table_ref[other]
            terms.append(terms_ref[other])
            d_x = own[0] - rows[0:1]
            d_y = own[1] - rows[1:2]
            d_z = own[2] - rows[2:3]
            squares = d_x * d_x + d_y * d_y + d_z * d_z
            weights.append(jnp.exp2(-squares).astype(jnp.bfloat16))
        sums = last_dims(jnp.concatenate(terms, axis=1), jnp.concatenate(weights, axis=1))
        sums = sums[0:4] + sums[4:8] + sums[8:12]
        place = pos_ref[:, at]
        speed = vel_ref[:, at]
        force = CONTACT_STIFF * (place * sums[0:1] - sums[1:4])

        cell_x, cell_y = cell_parts(cells_ref[step : step + 1, at], grid_y)
        hit = jnp.where(one_hot(cell_x, grid_x), 1.0, 0.0).astype(jnp.bfloat16)
        lines = jnp.dot(
            field_two_ref[...], jnp.concatenate([hit, hit], axis=0),
            preferred_element_type=jnp.float32,
        )
        pick = one_hot(cell_y, grid_y)
        gravity_x = jnp.sum(jnp.where(pick, lines[:grid_y], 0.0), axis=0, keepdims=True)
        gravity_y = jnp.sum(jnp.where(pick, lines[grid_y:], 0.0), axis=0, keepdims=True)
        accel = jnp.concatenate(
            [
                force[0:1]
                + gravity_x
                + 2.0 * ORBIT_FREQ * speed[1:2]
                + 3.0 * ORBIT_FREQ**2 * (place[0:1] + strip_x),
                force[1:2] + gravity_y - 2.0 * ORBIT_FREQ * speed[0:1],
                force[2:3] - ORBIT_FREQ**2 * (place[2:3] - 0.5),
            ],
            axis=0,
        )
        speed = speed + TIME_STEP * accel
        place = place + TIME_STEP * speed
        return at, place, speed

    def body(group, carry):
        for part in range(unroll):
            index = group * unroll + part
            at, place, speed = one_tile(index)
            if last:
                azi = lax.axis_index("azi")
                strip = nbr_ref[tile_count * LINKS + index]
                moved = lax.rem(azi - strip + azi_count + azi_count // 2, azi_count)
                moved = (moved - azi_count // 2).astype(jnp.float32)
                place = place + jnp.where(axis_ids == 1, moved, 0.0)
                to = pl.ds(pl.multiple_of(target_ref[index] * tile, tile), tile)
                out_ref[:, to] = jnp.concatenate([place, speed, mass_ref[:, at]], axis=0)
            else:
                pos_out[:, at] = place
                vel_out[:, at] = speed
        return carry

    lax.fori_loop(0, tile_count // unroll, body, 0)


def advance(step, counts, tile_count, grid_y, slots_out, numbers, slot_ids, target,
            place, speed, mass_row, received, cells, field):
    rad_count, azi_count = counts
    last = step == STEPS - 1
    tile = place.shape[1] // tile_count
    if last:
        out_shape = jax.ShapeDtypeStruct((7, slots_out * tile), jnp.float32)
        out_specs = VMEM
    else:
        out_shape = (jax.ShapeDtypeStruct(place.shape, jnp.float32),) * 2
        out_specs = (VMEM, VMEM)
    return pl.pallas_call(
        functools.partial(
            step_kernel, step, azi_count, rad_count, tile_count, grid_y, last, 2
        ),
        out_shape=out_shape,
        in_specs=[SMEM] * 3 + [VMEM] * 6,
        out_specs=out_specs,
        scratch_shapes=[
            pltpu.VMEM((tile_count + 4 * EDGE, 8, tile), jnp.float32),
            pltpu.VMEM((tile_count + 4 * EDGE, 16, tile), jnp.bfloat16),
            pltpu.VMEM((field.shape[0], 2 * field.shape[1]), jnp.bfloat16),
        ],
        name=f"advance_{step}",
        cost_estimate=pl.CostEstimate(
            flops=3 * 10**8, bytes_accessed=5 * 10**7, transcendentals=8 * 10**6
        ),
    )(numbers, slot_ids, target, place, speed, mass_row, received, cells, field)


def exact(left, right):
    return jnp.dot(left, right, precision=lax.Precision.HIGHEST)


def solve(density, rad_place, azi_place, rad_count, azi_count):
    _, grid_x, grid_y = density.shape
    size_x, size_y = grid_x * rad_count, grid_y * azi_count
    peers = rad_count * azi_count
    rows = size_y // peers
    basis_x, waves_x = real_basis(size_x)
    basis_y, waves_y = real_basis(size_y)
    slope_y = -0.5 * (np.roll(basis_y, -1, axis=1) - np.roll(basis_y, 1, axis=1))
    table_x = jnp.asarray(basis_x, jnp.float32)
    table_y = jnp.asarray(np.stack([basis_y.T, slope_y.T]), jnp.float32)
    own_y = lax.dynamic_slice_in_dim(table_y, azi_place * grid_y, grid_y, axis=1)
    flat = density.reshape(STEPS * grid_x, grid_y)
    partial = lax.dot_general(
        own_y[0], flat, (((0,), (1,)), ((), ())), precision=lax.Precision.HIGHEST
    )
    partial = partial.reshape(peers, rows, STEPS * grid_x)
    got = lax.all_to_all(partial, ("rad", "azi"), split_axis=0, concat_axis=0, tiled=True)
    lines = got.reshape(rad_count, azi_count, rows, STEPS, grid_x).sum(axis=1)
    lines = jnp.transpose(lines, (2, 1, 0, 3)).reshape(STEPS * rows, size_x)
    spectrum = lax.dot_general(
        lines, table_x, (((1,), (1,)), ((), ())), precision=lax.Precision.HIGHEST
    )
    eigen_x = jnp.asarray(4.0 * np.sin(np.pi * waves_x / size_x) ** 2, jnp.float32)
    eigen_y = jnp.asarray(4.0 * np.sin(np.pi * waves_y / size_y) ** 2, jnp.float32)
    own_eigen = lax.dynamic_slice_in_dim(
        eigen_y, (rad_place * azi_count + azi_place) * rows, rows, axis=0
    )
    total = eigen_x[None, :] + own_eigen[:, None]
    green = jnp.where(total == 0.0, 0.0, -GRAV_SCALE / jnp.where(total == 0.0, 1.0, total))
    spectrum = spectrum.reshape(STEPS, rows, size_x) * green[None]
    lines = exact(spectrum.reshape(STEPS * rows, size_x), table_x).reshape(STEPS, rows, size_x)
    slope = -0.5 * (jnp.roll(lines[0], -1, axis=1) - jnp.roll(lines[0], 1, axis=1))
    sent = jnp.concatenate([slope[None], lines], axis=0)
    sent = sent.reshape(STEPS + 1, rows, rad_count, grid_x)
    sent = jnp.transpose(sent, (2, 1, 0, 3)).reshape(rad_count, 1, rows, (STEPS + 1) * grid_x)
    sent = jnp.broadcast_to(sent, (rad_count, azi_count, rows, (STEPS + 1) * grid_x))
    sent = sent.reshape(peers, rows, (STEPS + 1) * grid_x)
    got = lax.all_to_all(sent, ("rad", "azi"), split_axis=0, concat_axis=0, tiled=True)
    got = got.reshape(size_y, (STEPS + 1) * grid_x)
    field = jnp.concatenate(
        [exact(own_y[0], got[:, :grid_x]), exact(own_y[1], got[:, grid_x : 2 * grid_x])], axis=0
    )
    final = exact(own_y[0], got[:, 2 * grid_x :]).T
    return field, final


def local(
    positions,
    velocities,
    masses,
    neighbours,
    shear_offsets,
    destinations,
    deposit_cells,
    old_potential,
):
    rad_count = lax.axis_size("rad")
    azi_count = lax.axis_size("azi")
    rad_place = lax.axis_index("rad")
    azi_place = lax.axis_index("azi")
    tile_count = neighbours.shape[0]
    tile = positions.shape[1] // tile_count
    grid_x, grid_y = old_potential.shape
    mass_row = masses[None]
    density = densities(deposit_cells, mass_row, grid_x, grid_y)

    span = EDGE * tile

    def edges_of(place, extra):
        head = jnp.concatenate([place[:, : 4 * span], mass_row[:, : 4 * span]], axis=0)
        sides = [head[:, side * span : (side + 1) * span] for side in (1, 0, 3, 2)]
        edges = jnp.stack(sides)
        if extra is not None:
            lines = [jnp.pad(line, (0, span - line.shape[0])) for line in extra]
            lines = jnp.stack(lines)[:, None]
            edges = jnp.concatenate(
                [edges, lines, jnp.zeros((4, 3, span), jnp.float32)], axis=1
            )
        return edges

    outer = (old_potential[-1], old_potential[0], old_potential[:, -1], old_potential[:, 0])
    received = exchange(edges_of(positions, outer), rad_count, azi_count, 0)
    before = lax.dynamic_index_in_dim(received, azi_place, 0, False)[4, :grid_y]
    after = lax.dynamic_index_in_dim(received, azi_count + azi_place, 0, False)[4, :grid_y]
    left = received[2 * azi_count, 4, :grid_x]
    right = received[2 * azi_count + 1, 4, :grid_x]
    tall = jnp.concatenate([before[None], old_potential, after[None]], axis=0)
    wide = jnp.concatenate([left[:, None], old_potential, right[:, None]], axis=1)
    grad_x = -(tall[2:] - tall[:-2]) * 0.5
    grad_y = -(wide[:, 2:] - wide[:, :-2]) * 0.5
    field = jnp.concatenate([grad_x.T, grad_y.T], axis=0)

    slot_cap = tile_count // 4
    slots_out = slot_cap * azi_count
    tile_ids = jnp.arange(tile_count, dtype=jnp.int32)
    sooner = (tile_ids[None, :] < tile_ids[:, None]) & (
        destinations[None, :] == destinations[:, None]
    )
    rank = jnp.sum(sooner.astype(jnp.int32), axis=1)
    target = destinations * slot_cap + rank
    numbers = jnp.concatenate([neighbours.reshape(-1), destinations])

    def slots_of(step):
        offsets = shear_offsets[step]
        shift_below = offsets[rad_place]
        shift_above = offsets[(rad_place + 1) % rad_count]
        return jnp.stack(
            [
                (azi_place - shift_below) % azi_count,
                azi_count + (azi_place + shift_above) % azi_count,
                jnp.int32(2 * azi_count),
                jnp.int32(2 * azi_count + 1),
            ]
        )

    counts = (rad_count, azi_count)
    place, speed = advance(
        0, counts, tile_count, grid_y, slots_out, numbers, slots_of(0), target,
        positions, velocities, mass_row, received, deposit_cells, field,
    )
    field, final = solve(density, rad_place, azi_place, rad_count, azi_count)
    received = exchange(edges_of(place, None), rad_count, azi_count, 1)
    packed = advance(
        1, counts, tile_count, grid_y, slots_out, numbers, slots_of(1), target,
        place, speed, mass_row, received, deposit_cells, field,
    )
    return (migrate(packed, azi_count, 2), final)


def solution(mesh):
    placed = (
        P(None, ("rad", "azi")),
        P(None, ("rad", "azi")),
        P(("rad", "azi")),
        P(("rad", "azi"), None),
        P(),
        P(("rad", "azi")),
        P(None, ("rad", "azi")),
        P("rad", "azi"),
    )
    return jax.shard_map(
        local,
        mesh=mesh,
        in_specs=placed,
        out_specs=(P(None, ("rad", "azi")), P("rad", "azi")),
        check_vma=False,
    )
```

time: 654 us -> 150 us (0.23); the launches traced: 645 us -> 149 us
  other arithmetic: 272 us -> 4.54 us
  local copies, waits for them, and re-layouts: 203 us -> 12.9 us
  Pallas kernels: 0 us -> 111 us
  waiting for transfers between devices: 54.6 us -> 0.01 us
  starting transfers between devices: 65 us -> 12 us
  blocking collectives: 26.3 us -> 0 us
  matrix products: 13.4 us -> 5.39 us
    scatter-add x8 -> x0, other arithmetic: 172 us -> none  [the longest x2 172 us: local(): jax.ops.segment_sum(masses, cells_now, num_segments=grid_x * grid_y)]
    gather x68 -> x0, local copies, waits for them, and re-layouts: 158 us -> none  [the longest x4 120 us: local(): gravity = jnp.take(grad_field, cells_now, axis=1)]
    pallas_call x0 -> x6, Pallas kernels: none -> 111 us  [the longest x2 69.6 us: advance(): pl.pallas_call(functools.partial(step_kernel, step, azi_count, rad_count,...]
    reduce_sum x129 -> x2, other arithmetic: 69.5 us -> 0.31 us  [the longest x1 0.17 us: local(): rank = jnp.sum(sooner.astype(jnp.int32), axis=1)]
    all_to_all x13 -> x2, waiting for transfers between devices: 41.5 us -> 0.01 us  [the longest x1 0.01 us: solve(): lax.all_to_all(partial, ('rad', 'azi'), split_axis=0, concat_axis=0, tile...]
    all_to_all x13 -> x2, starting transfers between devices: 47 us -> 12 us  [the longest x1 7.32 us: solve(): lax.all_to_all(partial, ('rad', 'azi'), split_axis=0, concat_axis=0, tile...]
    all_gather x2 -> x0, blocking collectives: 26.3 us -> none  [ghost_table(): all_rows = lax.all_gather(stacked[None], 'azi', axis=0, tiled=True)]
    ppermute x16 -> x0, starting transfers between devices: 18 us -> none  [the longest x8 11.1 us: shifted(): return lax.ppermute(value, axis, pairs)]
  transfers between devices with their start and end apart: 29 -> 2, of which waited for: 16 -> 0; matrix products, arithmetic and copies ran while one was open for 58% -> 6% of each run, Pallas kernels for 0% -> 37%
where the time goes in v1:
time: 150 us; the launch traced here: 149 us
  Pallas kernels  111 us (74%)
  local copies, waits for them, and re-layouts  12.9 us (9%)
  starting transfers between devices  12 us (8%)
  matrix products  5.39 us (4%)
  other arithmetic  4.54 us (3%)
  between operations  3.41 us (2%)
    pallas_call x2, Pallas kernels, advance(): pl.pallas_call(functools.partial(step_kernel, step, azi_count, rad_count,...  69.6 us
    pallas_call x2, Pallas kernels, exchange(): pl.pallas_call(functools.partial(exchange_kernel, rad_count, azi_count),...  19.9 us
    pallas_call x1, Pallas kernels, migrate(): pl.pallas_call(functools.partial(migrate_kernel, azi_count), out_shape=ja...  14.6 us
    all_to_all x1, starting transfers between devices, solve(): lax.all_to_all(partial, ('rad', 'azi'), split_axis=0, concat_axis=0, tile...  7.32 us
    pallas_call x1, Pallas kernels, densities(): pl.pallas_call(functools.partial(density_kernel, grid_x, grid_y, 1024), o...  6.52 us
    unnamed x24, local copies, waits for them, and re-layouts  5.77 us
    all_to_all x1, starting transfers between devices, solve(): lax.all_to_all(sent, ('rad', 'azi'), split_axis=0, concat_axis=0, tiled=T...  4.73 us
  transfers between devices with their start and end apart: 2, of which 0 were waited for; matrix products, arithmetic and copies ran while one was open for 6% of the time, Pallas kernels for 37%

profile of v1, /device:TPU:0, one launch (start us, length us, event | category | flops | bytes accessed | tf_op | source)
XLA Modules:
  0.0 148.8 jit_solution(6486739384034882590)
XLA Ops:
  0.6 6.5 %deposit.1 = f32[2,64,64]{2,1,0:T(8,128)} custom-call(s32[2,16384]{1,0:T(2,128)} %cells_ref.5, f32[1,16384]{1,0:T(1,128)} %bitcast.93), custom_call_target="tpu_custom_call" | custom-call | flops 400000000 | bytes 300000 | tf_op jit(solution)/shard_map/deposit/pallas_call | solution.py:82
  7.2 1.8 %fusion.3 = f32[32,8,128]{2,1,0:T(8,128)} fusion(f32[128,64,1]{1,0,2:T(8,128)} %bitcast.88, f32[2,256,256]{1,2,0:T(8,128)S(1)} %copy-done.2, s32[]{:T(128)S(6)} %select_n.70), kind=kOutput, calls=%fused_computation.6 | convolution fusion | flops 25165824 | bytes 294916 | tf_op jit(solution)/shard_map/dot_general | solution.py:353
  9.0 7.3 %all-to-all-start = ((f32[32,8,128]{2,1,0:T(8,128)}), f32[32,8,128]{2,1,0:T(8,128)S(1)}, u32[]{:S(2)}, u32[]{:S(2)}) async-start(f32[32,8,128]{2,1,0:T(8,128)} %fusion.3), calls=%async_computation | async-start | bytes 262144 | tf_op jit(solution)/shard_map/all_to_all | solution.py:357
  16.5 0.7 slice.154
  17.3 0.7 copy-done.7
  18.7 0.7 copy-done.4
  20.3 0.7 maximum_maximum_fusion.edges_ref
  21.0 10.4 %exchange_0.1.recv_ref = f32[10,8,512]{2,1,0:T(8,128)} custom-call(f32[4,8,512]{2,1,0:T(8,128)} %maximum_maximum_fusion.edges_ref), custom_call_target="tpu_custom_call" | custom-call | bytes 10000000 | tf_op jit(solution)/shard_map/exchange_0/pallas_call | solution.py:140
  31.4 0.8 slice_bitcast_fusion.5
  32.2 0.7 constant_dynamic-slice_fusion.1
  38.2 0.7 copy-done.9
  39.0 0.7 copy-done.5
  40.2 1.0 fusion
  42.5 0.7 broadcast_in_dim.34
  43.2 4.7 %all-to-all-start.1 = ((f32[32,8,192]{2,1,0:T(8,128)}), f32[32,8,192]{2,1,0:T(8,128)S(1)}, u32[]{:S(2)}, u32[]{:S(2)}) async-start(f32[32,8,192]{2,1,0:T(8,128)} %bitcast.42), calls=%async_computation.1 | async-start | bytes 524288 | tf_op jit(solution)/shard_map/all_to_all | solution.py:378
  47.9 0.7 pad_add_fusion
  49.2 34.7 %advance_0.1 = (f32[3,16384]{1,0:T(4,128)}, f32[3,16384]{1,0:T(4,128)}) custom-call(s32[640]{0:T(1024)} %copy-done.8, s32[4]{0:T(128)} %get-tuple-element.36.slot_ref, s32[128]{0:T(128)} %get-tuple-element.32.target_ref, f32[3,16384]{1,0:T(4,128)} %pos_ref.1, f32[3,16384]{1,0:T(4,128)} %vel_ref.1, f32[1,16384]{1,0:T(1,128)} %bitcast.95, ...), custom_call_target="tpu_custom_call" | custom-call | flops 300000000 | bytes 50000000 | tf_op jit(solution)/shard_map/advance_0/pallas_call | solution.py:318
  84.0 0.8 slice.140
  85.4 9.5 %exchange_1.1.recv_ref = f32[10,4,512]{2,1,0:T(4,128)} custom-call(f32[4,4,512]{2,1,0:T(4,128)} %pad_maximum_fusion.6.edges_ref), custom_call_target="tpu_custom_call" | custom-call | bytes 10000000 | tf_op jit(solution)/shard_map/exchange_1/pallas_call | solution.py:140
  94.9 1.0 fusion.2
  96.9 0.6 pad_maximum_fusion.1.field_ref
  97.5 34.8 %advance_1.1.packed_ref = f32[7,16384]{1,0:T(8,128)} custom-call(s32[640]{0:T(1024)} %copy-done.8, s32[4]{0:T(128)} %get-tuple-element.37.slot_ref, s32[128]{0:T(128)} %get-tuple-element.32.target_ref, f32[3,16384]{1,0:T(4,128)} %get-tuple-element.4.pos_ref, f32[3,16384]{1,0:T(4,128)} %get-tuple-element.5.vel_ref, f32[1,16384]{1,0:T(1,128)} %bitcast.96, ...), custom_call_target="tpu_custom_call" | custom-call | flops 300000000 | bytes 50000000 | tf_op jit(solution)/shard_map/advance_1/pallas_call | solution.py:318
  132.4 14.6 %migrate.1 = f32[7,16384]{1,0:T(8,128)} custom-call(f32[7,16384]{1,0:T(8,128)} %advance_1.1.packed_ref), custom_call_target="tpu_custom_call" | custom-call | bytes 40000000 | tf_op jit(solution)/shard_map/migrate/pallas_call | solution.py:183
  146.9 1.9 %copy.90 = f32[7,16384]{1,0:T(8,128)} copy(f32[7,16384]{1,0:T(8,128)} %migrate.1) | data formatting | bytes 917504
  (67 shorter events, 8.7 us)
Async XLA Ops:
  0.6 6.5 %copy-start.2 = (f32[2,256,256]{1,2,0:T(8,128)S(1)}, f32[2,256,256]{1,2,0:T(8,128)}, u32[]{:S(2)}) copy-start(f32[2,256,256]{1,2,0:T(8,128)} %constant.94.clone) | copy-start | bytes 1572868
  9.0 7.3 %copy-start.3 = (f32[64,64]{1,0:T(8,128)S(1)}, f32[64,64]{1,0:T(8,128)}, u32[]{:S(2)}) copy-start(f32[64,64]{1,0:T(8,128)} %param.19) | copy-start | bytes 49156
  9.0 30.7 %all-to-all-start = ((f32[32,8,128]{2,1,0:T(8,128)}), f32[32,8,128]{2,1,0:T(8,128)S(1)}, u32[]{:S(2)}, u32[]{:S(2)}) async-start(f32[32,8,128]{2,1,0:T(8,128)} %fusion.3), calls=%async_computation | async-start | bytes 262144 | tf_op jit(solution)/shard_map/all_to_all | solution.py:357
  17.3 0.7 copy-start.7
  18.0 0.7 copy-start.6
  18.7 0.7 copy-start.4
  19.5 0.8 slice-start
  31.4 8.8 %copy-start.1 = (f32[512,512,1]{1,0,2:T(8,128)S(1)}, f32[512,512,1]{1,0,2:T(8,128)}, u32[]{:S(2)}) copy-start(f32[512,512,1]{1,0,2:T(8,128)} %constant.105) | copy-start | bytes 3145732
  33.9 0.6 copy-start.8
  38.2 0.7 copy-start.9
  39.0 0.7 copy-start.5
  39.6 1.5 %copy-start = (f32[512,512]{1,0:T(8,128)S(1)}, f32[512,512]{1,0:T(8,128)}, u32[]{:S(2)}) copy-start(f32[512,512]{1,0:T(8,128)} %constant.93.clone) | copy-start | bytes 3145732
  43.2 51.7 %all-to-all-start.1 = ((f32[32,8,192]{2,1,0:T(8,128)}), f32[32,8,192]{2,1,0:T(8,128)S(1)}, u32[]{:S(2)}, u32[]{:S(2)}) async-start(f32[32,8,192]{2,1,0:T(8,128)} %bitcast.42), calls=%async_computation.1 | async-start | bytes 524288 | tf_op jit(solution)/shard_map/all_to_all | solution.py:378

commit v2 on v1

--- a/solution.py
+++ b/solution.py
@@ -18,6 +18,7 @@
 INV_WIDTH = 4.0
 GRAV_SCALE = 0.01
 SCALE = math.sqrt(INV_WIDTH * math.log2(math.e))
+UNROLL = 8
 MESH = pl.DeviceIdType.MESH
 VMEM = pl.BlockSpec(memory_space=pltpu.VMEM)
 SMEM = pl.BlockSpec(memory_space=pltpu.SMEM)
@@ -55,8 +56,12 @@
     )
 
 
-def density_kernel(grid_x, grid_y, chunk, cells_ref, mass_ref, out_ref):
+def density_kernel(
+    counts, grid_x, grid_y, chunk, cells_ref, mass_ref, edges_ref, out_ref, recv_ref, *sems
+):
     count = mass_ref.shape[1] // chunk
+    edges = Edges(*counts, edges_ref, recv_ref, *sems)
+    edges.greet()
 
     def body(index, sums):
         at = pl.ds(pl.multiple_of(index * chunk, chunk), chunk)
@@ -73,80 +78,111 @@
         return tuple(new)
 
     zero = jnp.zeros((2 * grid_x, grid_y), jnp.float32)
-    sums = lax.fori_loop(0, count, body, (zero,) * STEPS)
+    sums = lax.fori_loop(0, count // 4, body, (zero,) * STEPS)
+    edges.start()
+    sums = lax.fori_loop(count // 4, count, body, sums)
     for step in range(STEPS):
         out_ref[step] = sums[step][:grid_x] + sums[step][grid_x:]
-
-
-def densities(cells, mass_row, grid_x, grid_y):
+    edges.finish()
+
+
+def densities(cells, mass_row, edges, counts, grid_x, grid_y):
+    slots = 2 * counts[1] + 2
     return pl.pallas_call(
-        functools.partial(density_kernel, grid_x, grid_y, 1024),
-        out_shape=jax.ShapeDtypeStruct((STEPS, grid_x, grid_y), jnp.float32),
-        in_specs=[VMEM, VMEM],
-        out_specs=VMEM,
+        functools.partial(density_kernel, counts, grid_x, grid_y, 1024),
+        out_shape=(
+            jax.ShapeDtypeStruct((STEPS, grid_x, grid_y), jnp.float32),
+            jax.ShapeDtypeStruct((slots,) + edges.shape[1:], jnp.float32),
+        ),
+        in_specs=[VMEM, VMEM, VMEM],
+        out_specs=(VMEM, VMEM),
+        scratch_shapes=edge_sems(slots),
+        compiler_params=pltpu.CompilerParams(collective_id=0, has_side_effects=True),
         name="deposit",
         cost_estimate=pl.CostEstimate(flops=4 * 10**8, bytes_accessed=3 * 10**5, transcendentals=0),
-    )(cells, mass_row)
-
-
-def exchange_kernel(rad_count, azi_count, edges_ref, out_ref, send_sem, recv_sem):
-    rad = lax.axis_index("rad")
-    azi = lax.axis_index("azi")
-    above = lax.rem(rad + 1, rad_count)
-    below = lax.rem(rad + rad_count - 1, rad_count)
-    right = lax.rem(azi + 1, azi_count)
-    left = lax.rem(azi + azi_count - 1, azi_count)
-    partners = [(above, other) for other in range(azi_count)]
-    partners += [(below, other) for other in range(azi_count)]
-    partners += [(rad, right), (rad, left)]
-    barrier = pltpu.get_barrier_semaphore()
-    for partner in partners:
-        pl.semaphore_signal(barrier, inc=1, device_id=partner, device_id_type=MESH)
-    pl.semaphore_wait(barrier, len(partners))
-    copies = []
-    for index, partner in enumerate(partners):
-        if index < azi_count:
-            source, slot = 0, azi
-        elif index < 2 * azi_count:
-            source, slot = 1, azi_count + azi
-        else:
-            source = slot = index - 2 * azi_count
-            source, slot = 2 + source, 2 * azi_count + slot
-        copy = pltpu.make_async_remote_copy(
-            src_ref=edges_ref.at[source],
-            dst_ref=out_ref.at[slot],
-            send_sem=send_sem.at[index],
-            recv_sem=recv_sem.at[slot],
-            device_id=partner,
-            device_id_type=MESH,
-        )
-        copy.start()
-        copies.append(copy)
-    for index, partner in enumerate(partners):
-        pltpu.make_async_remote_copy(
-            src_ref=edges_ref.at[0],
-            dst_ref=out_ref.at[index],
-            send_sem=send_sem.at[index],
-            recv_sem=recv_sem.at[index],
-            device_id=partner,
-            device_id_type=MESH,
-        ).wait_recv()
-    for copy in copies:
-        copy.wait_send()
-
-
-def exchange(edges, rad_count, azi_count, ident):
-    slots = 2 * azi_count + 2
+    )(cells, mass_row, edges)
+
+
+def exchange_kernel(counts, edges_ref, out_ref, *sems):
+    edges = Edges(*counts, edges_ref, out_ref, *sems)
+    edges.greet()
+    edges.start()
+    edges.finish()
+
+
+def exchange(edges, counts, ident):
+    slots = 2 * counts[1] + 2
     return pl.pallas_call(
-        functools.partial(exchange_kernel, rad_count, azi_count),
+        functools.partial(exchange_kernel, counts),
         out_shape=jax.ShapeDtypeStruct((slots,) + edges.shape[1:], jnp.float32),
         in_specs=[VMEM],
         out_specs=VMEM,
-        scratch_shapes=[pltpu.SemaphoreType.DMA((slots,)), pltpu.SemaphoreType.DMA((slots,))],
+        scratch_shapes=edge_sems(slots),
         compiler_params=pltpu.CompilerParams(collective_id=ident, has_side_effects=True),
-        name=f"exchange_{ident}",
+        name="exchange",
         cost_estimate=pl.CostEstimate(flops=0, bytes_accessed=10**7, transcendentals=0),
     )(edges)
+
+
+class Edges:
+    def __init__(self, rad_count, azi_count, edges_ref, out_ref, send_sem, recv_sem):
+        rad, azi = lax.axis_index("rad"), lax.axis_index("azi")
+        above = lax.rem(rad + 1, rad_count)
+        below = lax.rem(rad + rad_count - 1, rad_count)
+        right = lax.rem(azi + 1, azi_count)
+        left = lax.rem(azi + azi_count - 1, azi_count)
+        self.partners = [(above, other) for other in range(azi_count)]
+        self.partners += [(below, other) for other in range(azi_count)]
+        self.partners += [(rad, right), (rad, left)]
+        self.copies = []
+        for index, partner in enumerate(self.partners):
+            if index < azi_count:
+                source, slot = 0, azi
+            elif index < 2 * azi_count:
+                source, slot = 1, azi_count + azi
+            else:
+                source, slot = 2 + index - 2 * azi_count, index
+            self.copies.append(
+                pltpu.make_async_remote_copy(
+                    src_ref=edges_ref.at[source],
+                    dst_ref=out_ref.at[slot],
+                    send_sem=send_sem.at[index],
+                    recv_sem=recv_sem.at[slot],
+                    device_id=partner,
+                    device_id_type=MESH,
+                )
+            )
+        self.arrivals = [
+            pltpu.make_async_remote_copy(
+                src_ref=edges_ref.at[0],
+                dst_ref=out_ref.at[index],
+                send_sem=send_sem.at[index],
+                recv_sem=recv_sem.at[index],
+                device_id=partner,
+                device_id_type=MESH,
+            )
+            for index, partner in enumerate(self.partners)
+        ]
+
+    def greet(self):
+        barrier = pltpu.get_barrier_semaphore()
+        for partner in self.partners:
+            pl.semaphore_signal(barrier, inc=1, device_id=partner, device_id_type=MESH)
+
+    def start(self):
+        pl.semaphore_wait(pltpu.get_barrier_semaphore(), len(self.partners))
+        for copy in self.copies:
+            copy.start()
+
+    def finish(self):
+        for arrival in self.arrivals:
+            arrival.wait_recv()
+        for copy in self.copies:
+            copy.wait_send()
+
+
+def edge_sems(slots):
+    return [pltpu.SemaphoreType.DMA((slots,)), pltpu.SemaphoreType.DMA((slots,))]
 
 
 def migrate_kernel(azi_count, packed_ref, out_ref, send_sem, recv_sem, local_sem):
@@ -201,12 +237,13 @@
     nbr_ref, slot_ref, target_ref, pos_ref, vel_ref, mass_ref, recv_ref, cells_ref, field_ref,
     *rest,
 ):
+    tile = pos_ref.shape[1] // tile_count
+    rad, azi = lax.axis_index("rad"), lax.axis_index("azi")
     if last:
         out_ref, table_ref, terms_ref, field_two_ref = rest
     else:
         pos_out, vel_out, table_ref, terms_ref, field_two_ref = rest
-    tile = pos_ref.shape[1] // tile_count
-    strip_x = (lax.axis_index("rad") - rad_count // 2).astype(jnp.float32)
+    strip_x = (rad - rad_count // 2).astype(jnp.float32)
     grid_x = field_ref.shape[1]
     high, low = split_two(field_ref[...])
     field_two_ref[...] = jnp.concatenate([high, low], axis=1).astype(jnp.bfloat16)
@@ -214,8 +251,15 @@
         out_ref[...] = jnp.zeros_like(out_ref)
 
     def enter(index, place, mass):
+        scaled = place * SCALE
         table_ref[index] = jnp.concatenate(
-            [place * SCALE, jnp.zeros((5, tile), jnp.float32)], axis=0
+            [
+                scaled,
+                -jnp.sum(scaled * scaled, axis=0, keepdims=True),
+                scaled + scaled,
+                jnp.zeros((1, tile), jnp.float32),
+            ],
+            axis=0,
         )
         rows = jnp.concatenate([mass, place * mass], axis=0)
         first = rows.astype(jnp.bfloat16).astype(jnp.float32)
@@ -243,17 +287,15 @@
     def one_tile(index):
         at = pl.ds(pl.multiple_of(index * tile, tile), tile)
         turned = jnp.transpose(table_ref[index])
-        own = [jnp.broadcast_to(turned[:, axis : axis + 1], (tile, tile)) for axis in range(3)]
+        own = [jnp.broadcast_to(turned[:, axis : axis + 1], (tile, tile)) for axis in range(4)]
         weights, terms = [], []
         for link in range(LINKS):
             other = nbr_ref[index * LINKS + link]
             rows = table_ref[other]
             terms.append(terms_ref[other])
-            d_x = own[0] - rows[0:1]
-            d_y = own[1] - rows[1:2]
-            d_z = own[2] - rows[2:3]
-            squares = d_x * d_x + d_y * d_y + d_z * d_z
-            weights.append(jnp.exp2(-squares).astype(jnp.bfloat16))
+            power = own[0] * rows[4:5] + own[1] * rows[5:6] + own[2] * rows[6:7]
+            power = power + (own[3] + rows[3:4])
+            weights.append(jnp.exp2(power).astype(jnp.bfloat16))
         sums = last_dims(jnp.concatenate(terms, axis=1), jnp.concatenate(weights, axis=1))
         sums = sums[0:4] + sums[4:8] + sums[8:12]
         place = pos_ref[:, at]
@@ -284,40 +326,55 @@
         place = place + TIME_STEP * speed
         return at, place, speed
 
+    def at_of(index):
+        return pl.ds(pl.multiple_of(index * tile, tile), tile)
+
+    if not last:
+
+        def body(group, carry):
+            for part in range(unroll):
+                at, place, speed = one_tile(group * unroll + part)
+                pos_out[:, at] = place
+                vel_out[:, at] = speed
+            return carry
+
+        lax.fori_loop(0, tile_count // unroll, body, 0)
+        return
+
+    def shifted(place, strip):
+        moved = lax.rem(azi - strip + azi_count + azi_count // 2, azi_count)
+        moved = (moved - azi_count // 2).astype(jnp.float32)
+        return place + jnp.where(axis_ids == 1, moved, 0.0)
+
     def body(group, carry):
         for part in range(unroll):
             index = group * unroll + part
             at, place, speed = one_tile(index)
-            if last:
-                azi = lax.axis_index("azi")
-                strip = nbr_ref[tile_count * LINKS + index]
-                moved = lax.rem(azi - strip + azi_count + azi_count // 2, azi_count)
-                moved = (moved - azi_count // 2).astype(jnp.float32)
-                place = place + jnp.where(axis_ids == 1, moved, 0.0)
-                to = pl.ds(pl.multiple_of(target_ref[index] * tile, tile), tile)
-                out_ref[:, to] = jnp.concatenate([place, speed, mass_ref[:, at]], axis=0)
-            else:
-                pos_out[:, at] = place
-                vel_out[:, at] = speed
+            place = shifted(place, nbr_ref[tile_count * LINKS + index])
+            out_ref[:, at_of(target_ref[index])] = jnp.concatenate(
+                [place, speed, mass_ref[:, at]], axis=0
+            )
         return carry
 
     lax.fori_loop(0, tile_count // unroll, body, 0)
-
 
 def advance(step, counts, tile_count, grid_y, slots_out, numbers, slot_ids, target,
             place, speed, mass_row, received, cells, field):
     rad_count, azi_count = counts
     last = step == STEPS - 1
     tile = place.shape[1] // tile_count
+    params = pltpu.CompilerParams()
     if last:
         out_shape = jax.ShapeDtypeStruct((7, slots_out * tile), jnp.float32)
         out_specs = VMEM
+        more = []
     else:
         out_shape = (jax.ShapeDtypeStruct(place.shape, jnp.float32),) * 2
-        out_specs = (VMEM, VMEM)
+        out_specs = (VMEM,) * 2
+        more = []
     return pl.pallas_call(
         functools.partial(
-            step_kernel, step, azi_count, rad_count, tile_count, grid_y, last, 2
+            step_kernel, step, azi_count, rad_count, tile_count, grid_y, last, UNROLL
         ),
         out_shape=out_shape,
         in_specs=[SMEM] * 3 + [VMEM] * 6,
@@ -326,7 +383,9 @@
             pltpu.VMEM((tile_count + 4 * EDGE, 8, tile), jnp.float32),
             pltpu.VMEM((tile_count + 4 * EDGE, 16, tile), jnp.bfloat16),
             pltpu.VMEM((field.shape[0], 2 * field.shape[1]), jnp.bfloat16),
-        ],
+        ]
+        + more,
+        compiler_params=params,
         name=f"advance_{step}",
         cost_estimate=pl.CostEstimate(
             flops=3 * 10**8, bytes_accessed=5 * 10**7, transcendentals=8 * 10**6
@@ -402,8 +461,6 @@
     tile = positions.shape[1] // tile_count
     grid_x, grid_y = old_potential.shape
     mass_row = masses[None]
-    density = densities(deposit_cells, mass_row, grid_x, grid_y)
-
     span = EDGE * tile
 
     def edges_of(place, extra):
@@ -419,7 +476,10 @@
         return edges
 
     outer = (old_potential[-1], old_potential[0], old_potential[:, -1], old_potential[:, 0])
-    received = exchange(edges_of(positions, outer), rad_count, azi_count, 0)
+    counts = (rad_count, azi_count)
+    density, received = densities(
+        deposit_cells, mass_row, edges_of(positions, outer), counts, grid_x, grid_y
+    )
     before = lax.dynamic_index_in_dim(received, azi_place, 0, False)[4, :grid_y]
     after = lax.dynamic_index_in_dim(received, azi_count + azi_place, 0, False)[4, :grid_y]
     left = received[2 * azi_count, 4, :grid_x]
@@ -453,13 +513,12 @@
             ]
         )
 
-    counts = (rad_count, azi_count)
     place, speed = advance(
         0, counts, tile_count, grid_y, slots_out, numbers, slots_of(0), target,
         positions, velocities, mass_row, received, deposit_cells, field,
     )
     field, final = solve(density, rad_place, azi_place, rad_count, azi_count)
-    received = exchange(edges_of(place, None), rad_count, azi_count, 1)
+    received = exchange(edges_of(place, None), counts, 1)
     packed = advance(
         1, counts, tile_count, grid_y, slots_out, numbers, slots_of(1), target,
         place, speed, mass_row, received, deposit_cells, field,

time: 150 us -> 125 us (0.83)
  Pallas kernels: 111 us -> 85.7 us
    pallas_call x2, Pallas kernels: 69.6 us -> 49.6 us  [advance(): pl.pallas_call(functools.partial(step_kernel, step, azi_count, rad_count,...]
    pallas_call x3 -> x2, Pallas kernels: 26.4 us -> 21.6 us  [the longest x1 12.1 us: densities(): pl.pallas_call(functools.partial(density_kernel, counts, grid_x, grid_y,...]
    all_to_all x1, starting transfers between devices: 7.32 us -> 4.73 us  [solve(): lax.all_to_all(partial, ('rad', 'azi'), split_axis=0, concat_axis=0, tile...]
  transfers between devices with their start and end apart: 2 -> 2, of which waited for: 0 -> 0; matrix products, arithmetic and copies ran while one was open for 6% -> 6% of each run, Pallas kernels for 37% -> 28%
where the time goes in v2:
time: 125 us; the launch traced here: 124 us
  Pallas kernels  85.7 us (69%)
  local copies, waits for them, and re-layouts  14 us (11%)
  starting transfers between devices  10.6 us (8%)
  matrix products  5.4 us (4%)
  other arithmetic  4.46 us (4%)
  between operations  3.68 us (3%)
    pallas_call x2, Pallas kernels, advance(): pl.pallas_call(functools.partial(step_kernel, step, azi_count, rad_count,...  49.6 us
    pallas_call x1, Pallas kernels, migrate(): pl.pallas_call(functools.partial(migrate_kernel, azi_count), out_shape=ja...  14.6 us
    pallas_call x1, Pallas kernels, densities(): pl.pallas_call(functools.partial(density_kernel, counts, grid_x, grid_y,...  12.1 us
    pallas_call x1, Pallas kernels, exchange(): pl.pallas_call(functools.partial(exchange_kernel, counts), out_shape=jax....  9.5 us
    all_to_all x1, starting transfers between devices, solve(): lax.all_to_all(sent, ('rad', 'azi'), split_axis=0, concat_axis=0, tiled=T...  5.83 us
    unnamed x24, local copies, waits for them, and re-layouts  5.08 us
    all_to_all x1, starting transfers between devices, solve(): lax.all_to_all(partial, ('rad', 'azi'), split_axis=0, concat_axis=0, tile...  4.73 us
    dot_general x4, matrix products, exact(): return jnp.dot(left, right, precision=lax.Precision.HIGHEST)  2.62 us
  transfers between devices with their start and end apart: 2, of which 0 were waited for; matrix products, arithmetic and copies ran while one was open for 6% of the time, Pallas kernels for 28%

profile of v2, /device:TPU:0, one launch (start us, length us, event | category | flops | bytes accessed | tf_op | source)
XLA Modules:
  0.0 123.8 jit_solution(4579115730761461813)
XLA Ops:
  0.6 0.7 slice_bitcast_fusion.7
  1.3 1.0 slice_reduce_fusion.1
  2.5 0.7 slice.154
  3.2 0.7 slice-done
  3.9 0.7 maximum_maximum_fusion.edges_ref
  4.6 12.1 %deposit.1 = (f32[2,64,64]{2,1,0:T(8,128)}, f32[10,8,512]{2,1,0:T(8,128)}) custom-call(s32[2,16384]{1,0:T(2,128)} %cells_ref.5, f32[1,16384]{1,0:T(1,128)} %bitcast.94, f32[4,8,512]{2,1,0:T(8,128)} %maximum_maximum_fusion.edges_ref), custom_call_target="tpu_custom_call" | custom-call | flops 400000000 | bytes 300000 | tf_op jit(solution)/shard_map/deposit/pallas_call | solution.py:91
  16.7 1.8 %fusion.3 = f32[32,8,128]{2,1,0:T(8,128)} fusion(f32[128,64,1]{1,0,2:T(8,128)} %bitcast.88, f32[2,256,256]{1,2,0:T(8,128)S(1)} %copy-done.2, s32[]{:T(128)S(6)} %select_n.70), kind=kOutput, calls=%fused_computation.6 | convolution fusion | flops 25165824 | bytes 294916 | tf_op jit(solution)/shard_map/dot_general | solution.py:412
  18.5 4.7 %all-to-all-start = ((f32[32,8,128]{2,1,0:T(8,128)}), f32[32,8,128]{2,1,0:T(8,128)S(1)}, u32[]{:S(2)}, u32[]{:S(2)}) async-start(f32[32,8,128]{2,1,0:T(8,128)} %fusion.3), calls=%async_computation | async-start | bytes 262144 | tf_op jit(solution)/shard_map/all_to_all | solution.py:416
  25.0 0.8 slice_bitcast_fusion.5
  25.7 0.7 constant_dynamic-slice_fusion.1
  30.0 0.7 constant_dynamic-slice_fusion.5
  32.1 0.7 copy-done.9
  32.8 0.7 copy-done.5
  34.1 1.0 fusion
  36.4 0.7 broadcast_in_dim.34
  37.1 5.8 %all-to-all-start.1 = ((f32[32,8,192]{2,1,0:T(8,128)}), f32[32,8,192]{2,1,0:T(8,128)S(1)}, u32[]{:S(2)}, u32[]{:S(2)}) async-start(f32[32,8,192]{2,1,0:T(8,128)} %bitcast.42), calls=%async_computation.1 | async-start | bytes 524288 | tf_op jit(solution)/shard_map/all_to_all | solution.py:437
  42.9 0.7 pad_add_fusion
  44.2 24.6 %advance_0.1 = (f32[3,16384]{1,0:T(4,128)}, f32[3,16384]{1,0:T(4,128)}) custom-call(s32[640]{0:T(1024)} %copy-done.8, s32[4]{0:T(128)} %get-tuple-element.40.slot_ref, s32[128]{0:T(128)} %get-tuple-element.36.target_ref, f32[3,16384]{1,0:T(4,128)} %pos_ref.1, f32[3,16384]{1,0:T(4,128)} %vel_ref.1, f32[1,16384]{1,0:T(1,128)} %bitcast.95, ...), custom_call_target="tpu_custom_call" | custom-call | flops 300000000 | bytes 50000000 | tf_op jit(solution)/shard_map/advance_0/pallas_call | solution.py:375
  68.8 0.8 slice.140
  70.2 9.5 %exchange.1.recv_ref = f32[10,4,512]{2,1,0:T(4,128)} custom-call(f32[4,4,512]{2,1,0:T(4,128)} %pad_maximum_fusion.6.edges_ref), custom_call_target="tpu_custom_call" | custom-call | bytes 10000000 | tf_op jit(solution)/shard_map/exchange/pallas_call | solution.py:115
  79.8 1.0 fusion.2
  82.4 25.0 %advance_1.1.packed_ref = f32[7,16384]{1,0:T(8,128)} custom-call(s32[640]{0:T(1024)} %copy-done.8, s32[4]{0:T(128)} %get-tuple-element.41.slot_ref, s32[128]{0:T(128)} %get-tuple-element.36.target_ref, f32[3,16384]{1,0:T(4,128)} %get-tuple-element.7.pos_ref, f32[3,16384]{1,0:T(4,128)} %get-tuple-element.8.vel_ref, f32[1,16384]{1,0:T(1,128)} %bitcast.96, ...), custom_call_target="tpu_custom_call" | custom-call | flops 300000000 | bytes 50000000 | tf_op jit(solution)/shard_map/advance_1/pallas_call | solution.py:375
  107.4 14.6 %migrate.1 = f32[7,16384]{1,0:T(8,128)} custom-call(f32[7,16384]{1,0:T(8,128)} %advance_1.1.packed_ref), custom_call_target="tpu_custom_call" | custom-call | bytes 40000000 | tf_op jit(solution)/shard_map/migrate/pallas_call | solution.py:219
  121.9 1.9 %copy.90 = f32[7,16384]{1,0:T(8,128)} copy(f32[7,16384]{1,0:T(8,128)} %migrate.1) | data formatting | bytes 917504
  (66 shorter events, 8.7 us)
Async XLA Ops:
  3.2 0.8 slice-start
  4.6 12.1 %copy-start.2 = (f32[2,256,256]{1,2,0:T(8,128)S(1)}, f32[2,256,256]{1,2,0:T(8,128)}, u32[]{:S(2)}) copy-start(f32[2,256,256]{1,2,0:T(8,128)} %constant.94.clone) | copy-start | bytes 1572868
  18.5 4.8 %copy-start.3 = (f32[64,64]{1,0:T(8,128)S(1)}, f32[64,64]{1,0:T(8,128)}, u32[]{:S(2)}) copy-start(f32[64,64]{1,0:T(8,128)} %param.19) | copy-start | bytes 49156
  18.5 15.1 %all-to-all-start = ((f32[32,8,128]{2,1,0:T(8,128)}), f32[32,8,128]{2,1,0:T(8,128)S(1)}, u32[]{:S(2)}, u32[]{:S(2)}) async-start(f32[32,8,128]{2,1,0:T(8,128)} %fusion.3), calls=%async_computation | async-start | bytes 262144 | tf_op jit(solution)/shard_map/all_to_all | solution.py:416
  23.3 0.9 copy-start.6
  23.4 0.7 copy-start.7
  24.1 0.7 copy-start.4
  25.0 9.1 %copy-start.1 = (f32[512,512,1]{1,0,2:T(8,128)S(1)}, f32[512,512,1]{1,0,2:T(8,128)}, u32[]{:S(2)}) copy-start(f32[512,512,1]{1,0,2:T(8,128)} %constant.105) | copy-start | bytes 3145732
  27.4 0.6 copy-start.8
  32.1 0.7 copy-start.9
  32.8 0.7 copy-start.5
  33.5 1.5 %copy-start = (f32[512,512]{1,0:T(8,128)S(1)}, f32[512,512]{1,0:T(8,128)}, u32[]{:S(2)}) copy-start(f32[512,512]{1,0:T(8,128)} %constant.93.clone) | copy-start | bytes 3145732
  37.1 42.7 %all-to-all-start.1 = ((f32[32,8,192]{2,1,0:T(8,128)}), f32[32,8,192]{2,1,0:T(8,128)S(1)}, u32[]{:S(2)}, u32[]{:S(2)}) async-start(f32[32,8,192]{2,1,0:T(8,128)} %bitcast.42), calls=%async_computation.1 | async-start | bytes 524288 | tf_op jit(solution)/shard_map/all_to_all | solution.py:437
